TPU v7x, 32 devices: a whole 2x2x4 slice. The times are simulated.
32 devices in a mesh: batch: 2 (over y), freq: 8 (over z, x), elem: 2 (over core).
Axes of the slice: x: 2, y: 2, z: 4, core: 2. Of those that a mesh axis runs over, the one named last changes fastest.
Arguments:
- flaw_cells: int32 [512], P('batch'), parts along dimension 0, may hold values from 0 to 255, each once
- flaw_blocks: int32 [16], P('batch'), parts along dimension 0, may hold values from 0 to 7, each once
- element_channel: int32 [256], P('elem'), may hold values from 0 to 255, each once
- focal_delay: float32 [256, 256], replicated, may hold values from 0 to 64
- beam_field: bfloat16 [128, 2, 256, 256], P('freq', None, 'elem'), may hold values from -0.125 to 0.125
- flaw_size: float32 [4, 128], P('batch'), parts along dimension 0, may hold values from 0.5 to 4
- flaw_slope: float32 [4, 128], P('batch'), parts along dimension 0, may hold values from 0.2 to 1
- noise_level: float32 [4, 128], P(('batch', 'elem'), 'freq'), parts along dimension 0, may hold values from 0.5 to 5
Outputs:
- flaw_peak: float32 [4, 128], P(('batch', 'elem'), 'freq'), parts along dimension 0
- detection: float32 [4, 128], P(('batch', 'elem'), 'freq'), parts along dimension 0
There are 2 independent parts, one for each index of `batch`. A program takes and returns all parts, laid end to end along the dimension named above; an argument that names none is the same for every part. Nothing has to cross between parts.
Inputs may be any that keep to these rules, and one draw needn't show every extreme that they name: `flaw_cells`: every site holds exactly one flaw. `flaw_blocks`: every scan block belongs to exactly one flaw group. `element_channel`: every channel drives exactly one element.
All inputs are finite; a program needn't handle non-finite values.
Results may differ from a plain program's by a relative error of at most 0.0011.
Values may be sent and summed in bfloat16 or wider, within the bound.
A program may use at most 64 MiB of HBM per device.

v0:
```python
import math
import jax
import jax.numpy as jnp
from jax import lax
from jax.sharding import PartitionSpec as P

W_DEV = 16
FG = 128
NB = 4
SB = 32
T_CAP = 1024
EDGE = 0.6
STEEP = 3.0
EPS = 1e-05


def kirchhoff(angular, flaw_size, flaw_slope):
    angles = angular[None, :, None] * (2.0 * flaw_size * flaw_slope)[:, None, :]
    real_part = flaw_size[:, None, :] * (1.0 + EDGE) * jnp.cos(angles)
    imag_part = flaw_size[:, None, :] * (EDGE - 1.0) * jnp.sin(angles)
    return (real_part, imag_part)


def focal_law(angular, delays):
    phases = angular[:, None, None, None] * delays[None]
    return jnp.concatenate([jnp.cos(phases), -jnp.sin(phases)], axis=-1).astype(jnp.bfloat16)


def field_matrix(fields):
    real_part = fields[:, 0]
    imag_part = fields[:, 1]
    upper_rows = jnp.concatenate([real_part, imag_part], axis=-1)
    lower_rows = jnp.concatenate([-imag_part, real_part], axis=-1)
    return jnp.concatenate([upper_rows, lower_rows], axis=1)


def combine(product, k_real, k_imag):
    columns = k_real.shape[-1]
    real_part = product[..., :columns]
    imag_part = product[..., columns:]
    scale_real = k_real[:, :, None, :]
    scale_imag = k_imag[:, :, None, :]
    return jnp.stack(
        [
            scale_real * real_part - scale_imag * imag_part,
            scale_real * imag_part + scale_imag * real_part,
        ],
        axis=2,
    )


def envelope_peak(spectra, row_count):
    groups, freq_total, planes, columns = spectra.shape
    sample_count = min(T_CAP, 2 * freq_total)
    time_block = min(128, sample_count)
    freq_index = jnp.arange(freq_total, dtype=jnp.int32)
    scaling = 1.0 / math.sqrt(freq_total)

    def advance(step_index, running):
        sample_times = step_index * time_block + jnp.arange(time_block, dtype=jnp.int32)
        phase_steps = freq_index[:, None] * sample_times[None, :] % (2 * freq_total)
        angles = phase_steps.astype(jnp.float32) * (math.pi / freq_total)
        cosine = jnp.cos(angles)
        sine_part = jnp.sin(angles)
        twiddle = jnp.stack(
            [jnp.stack([cosine, sine_part], axis=1), jnp.stack([-sine_part, cosine], axis=1)],
            axis=1,
        )
        twiddle_high = lax.optimization_barrier(twiddle.astype(jnp.bfloat16))
        twiddle_low = (twiddle - twiddle_high.astype(jnp.float32)).astype(jnp.bfloat16)
        signal = jnp.einsum(
            "gwcx,wckt->gkxt", spectra, twiddle_high, preferred_element_type=jnp.float32
        )
        signal = signal + jnp.einsum(
            "gwcx,wckt->gkxt", spectra, twiddle_low, preferred_element_type=jnp.float32
        )
        signal = signal * scaling
        magnitude = jnp.sqrt(signal[:, 0] * signal[:, 0] + signal[:, 1] * signal[:, 1])
        magnitude = magnitude.reshape(groups, row_count, columns // row_count, time_block)
        return jnp.maximum(running, jnp.max(magnitude, axis=(1, 3)))

    initial = jnp.zeros((groups, columns // row_count), jnp.float32)
    return lax.fori_loop(0, sample_count // time_block, advance, initial)


def regroup_peaks(moved):
    groups, freq_total, planes, row_count, flaw_count = moved.shape
    return envelope_peak(
        moved.reshape(groups, freq_total, planes, row_count * flaw_count), row_count
    )


def body(
    flaw_cells,
    flaw_blocks,
    element_channel,
    focal_delay,
    beam_field,
    flaw_size,
    flaw_slope,
    noise_level,
):
    freq_count = lax.axis_size("freq")
    freq_total = W_DEV * freq_count
    group_total = flaw_size.shape[0]
    row_total = NB * SB
    first_freq = lax.axis_index("freq") * W_DEV
    angular = (first_freq + jnp.arange(W_DEV, dtype=jnp.int32)).astype(jnp.float32) * (
        math.pi / freq_total
    )
    scan_rows = (
        flaw_blocks.reshape(group_total, NB)[:, :, None] * SB
        + jnp.arange(SB, dtype=jnp.int32)[None, None, :]
    ).reshape(group_total, row_total)
    delays = jnp.moveaxis(
        jnp.take(jnp.take(focal_delay, element_channel, axis=0), scan_rows, axis=1), 0, 2
    )
    fields = jnp.take(beam_field, flaw_cells, axis=3).reshape(
        W_DEV, 2, element_channel.shape[0], group_total, FG
    )
    k_real, k_imag = kirchhoff(angular, flaw_size, flaw_slope)
    focal_terms = focal_law(angular, delays)
    field_terms = field_matrix(fields)
    product = jnp.einsum(
        "wgre,wegf->gwrf", focal_terms, field_terms, preferred_element_type=jnp.float32
    )
    partial_value = combine(product, k_real, k_imag).astype(jnp.bfloat16)
    rounded_term = lax.optimization_barrier(partial_value).astype(jnp.float32)
    summed = lax.psum_scatter(
        rounded_term.astype(jnp.bfloat16), "elem", scatter_dimension=0, tiled=True
    )
    partial_peak = regroup_peaks(
        lax.all_to_all(summed, "freq", split_axis=3, concat_axis=1, tiled=True)
    )
    whole_peak = lax.pmax(partial_peak, "freq")
    columns = FG // freq_count
    flaw_peak = lax.dynamic_slice_in_dim(whole_peak, lax.axis_index("freq") * columns, columns, 1)
    detection = jax.nn.sigmoid(STEEP * (jnp.log(flaw_peak + EPS) - jnp.log(noise_level)))
    return (flaw_peak, detection)


def solution(mesh):
    in_specs = (
        P("batch"),
        P("batch"),
        P("elem"),
        P(),
        P("freq", None, "elem", None),
        P("batch", None),
        P("batch", None),
        P(("batch", "elem"), "freq"),
    )
    out_specs = (P(("batch", "elem"), "freq"), P(("batch", "elem"), "freq"))
    return jax.shard_map(body, mesh=mesh, in_specs=in_specs, out_specs=out_specs, check_vma=False)
```

profile of v0, /device:TPU:0, one launch (start us, length us, event | category | flops | bytes accessed | tf_op | source)
XLA Modules:
  0.0 130.7 jit_solution(10028995258592045228)
XLA Ops:
  7.2 0.7 compare_select_fusion.3
  7.9 1.2 compare_and_fusion
  9.1 0.7 broadcast_multiply_fusion.2
  10.1 0.7 compare_select_fusion
  10.8 0.7 and_bitcast_fusion
  11.4 3.5 %copy.28 = bf16[16,2,128,256]{2,0,3,1:T(8,128)(2,1)S(1)} copy(bf16[16,2,128,256]{3,2,1,0:T(8,128)(2,1)} %param.14) | data formatting | bytes 4194304 | tf_op args[4]
  14.9 2.3 %gather_fusion.2 = bf16[256,16,2,128]{3,1,2,0:T(8,128)(2,1)} fusion(bf16[16,2,128,256]{2,0,3,1:T(8,128)(2,1)S(1)} %copy.28, s32[1024]{0:T(1024)S(1)} %pad_clamp_fusion), kind=kCustom, calls=%fused_computation.2 | custom fusion | bytes 4195328 | tf_op jit(solution)/shard_map/jit(_take)/gather | solution.py:118
  17.2 3.5 %copy.30 = bf16[16,2,128,2,128]{4,2,0,3,1:T(8,128)(2,1)S(1)} copy(bf16[16,2,128,2,128]{2,0,1,4,3:T(8,128)(2,1)} %bitcast.85) | data formatting | bytes 4194304 | tf_op jit(solution)/shard_map/jit(_take)/gather | solution.py:118
  21.3 0.8 gather_fusion
  22.1 1.4 %broadcast_select_fusion.3 = f32[128,256]{1,0:T(8,128)} fusion(f32[128,256]{1,0:T(8,128)S(1)} %gather_fusion, pred[128]{0:T(512)(128)(4,1)} %compare_and_fusion), kind=kLoop, calls=%fused_computation.64 | loop fusion | flops 32768 | bytes 262272 | tf_op jit(solution)/shard_map/jit(_take)/select_n | solution.py:116
  23.5 1.0 copy.27
  25.0 1.3 %gather_fusion.1 = f32[256,128]{1,0:T(8,128)} fusion(f32[128,256]{0,1:T(8,128)S(1)} %copy.27, s32[1024]{0:T(1024)S(1)} %pad_clamp_fusion.1), kind=kCustom, calls=%fused_computation.1 | custom fusion | bytes 263168 | tf_op jit(solution)/shard_map/jit(_take)/gather | solution.py:116
  26.3 1.0 broadcast_select_fusion.2
  27.3 7.8 %fusion.30 = (bf16[16,2,128,128]{3,2,0,1:T(8,128)(2,1)S(1)}, bf16[16,2,128,128]{3,2,0,1:T(8,128)(2,1)S(1)}) fusion(f32[2,128,128]{2,1,0:T(8,128)S(1)} %broadcast_select_fusion.2, f32[16]{0:T(128)S(1)} %convert_multiply_fusion), kind=kLoop, calls=%fused_computation.49 | loop fusion | flops 2097152 | bytes 2228288 | tf_op jit(solution)/shard_map/convert.4
  35.1 0.7 broadcast_multiply_fusion.1
  36.0 1.4 %fusion.22 = f32[2,16,128,256]{3,2,1,0:T(8,128)S(1)} fusion(bf16[16,128,2,128]{3,1,0,2:T(8,128)(2,1)S(1)} %get-tuple-element.144, bf16[16,128,2,128]{3,1,0,2:T(8,128)(2,1)S(1)} %fusion.42, bf16[16,128,2,128]{3,1,0,2:T(8,128)(2,1)S(1)} %get-tuple-element.143, bf16[16,2,128,128]{3,2,0,1:T(8,128)(2,1)S(1)} %get-tuple-element.146, ...), kind=kOutput, calls=%fused_computation.39 | convolution fusion | flops 557842432 | bytes 9437184 | tf_op jit(solution)/shard_map/wgre,wegf->gwrf/dot_general | solution.py:124
  38.1 1.5 %pad_maximum_fusion.1 = bf16[2,16,2,128,128]{4,3,1,0,2:T(8,128)(2,1)} fusion(bf16[2,16,1,128,128]{4,3,1,0,2:T(8,128)(2,1)S(1)} %get-tuple-element.142, bf16[2,16,1,128,128]{4,3,1,0,2:T(8,128)(2,1)S(1)} %get-tuple-element.141), kind=kLoop, calls=%fused_computation.55 | loop fusion | flops 1048576 | bytes 4194304 | tf_op jit(solution)/shard_map/stack | solution.py:43
  40.8 22.9 %all-reduce.3.cloned.1.call-done = bf16[2,16,2,128,128]{4,3,1,0,2:T(8,128)(2,1)} async-done(((bf16[2,16,2,128,128]{4,3,1,0,2:T(8,128)(2,1)}), bf16[2,16,2,128,128]{4,3,1,0,2:T(8,128)(2,1)}) %all-reduce.3.cloned.1.call-update) | async-done | bytes 2097168
  63.6 1.9 %constant_dynamic-slice_fusion = bf16[1,16,2,128,128]{4,3,1,0,2:T(8,128)(2,1)S(1)} fusion(bf16[2,16,2,128,128]{4,3,1,0,2:T(8,128)(2,1)} %all-reduce.3.cloned.1.call-done, u32[]{:T(128)} %bitcast.34), kind=kLoop, calls=%fused_computation.81 | loop fusion | bytes 2097156
  65.6 1.7 %copy.31 = bf16[1,16,2,128,128]{4,1,0,2,3:T(8,128)(2,1)} copy(bf16[1,16,2,128,128]{4,3,1,0,2:T(8,128)(2,1)S(1)} %constant_dynamic-slice_fusion) | data formatting | bytes 2097152 | tf_op jit(solution)/shard_map/reduce_scatter | solution.py:129
  67.2 5.8 %all-to-all-start = ((bf16[1,16,2,128,128]{4,1,0,2,3:T(8,128)(2,1)}), bf16[1,16,2,128,128]{4,1,0,2,3:T(8,128)(2,1)S(1)}, u32[]{:S(2)}, u32[]{:S(2)}) async-start(bf16[1,16,2,128,128]{4,1,0,2,3:T(8,128)(2,1)} %copy.31), calls=%async_computation | async-start | bytes 2097152 | tf_op jit(solution)/shard_map/all_to_all | solution.py:133
  73.0 26.2 %all-to-all-done = bf16[1,16,2,128,128]{4,1,0,2,3:T(8,128)(2,1)S(1)} async-done(((bf16[1,16,2,128,128]{4,1,0,2,3:T(8,128)(2,1)}), bf16[1,16,2,128,128]{4,1,0,2,3:T(8,128)(2,1)S(1)}, u32[]{:S(2)}, u32[]{:S(2)}) %all-to-all-start) | async-done | bytes 1048608 | tf_op jit(solution)/shard_map/all_to_all | solution.py:133
  100.2 3.5 %while.16 = (s32[]{:T(128)}, f32[1,128]{1,0:T(1,128)S(1)}, bf16[1,128,2,2048]{3,1,2,0:T(8,128)(2,1)S(1)}, s32[]{:T(128)}, s32[]{:T(128)}, /*index=5*/s32[]{:T(128)}) while((s32[]{:T(128)}, f32[1,128]{1,0:T(1,128)S(1)}, bf16[1,128,2,2048]{3,1,2,0:T(8,128)(2,1)S(1)}, s32[]{:T(128)}, s32[]{:T(128)}, /*index=5*/s32[]{:T(128)}) %tuple.58), condition=%wide.region_4.5_spmd.clone, body=%wide.region_1.4_spmd.clone.sunk | while | flops 539607296 | bytes 12078175 | solution.py:83
  103.7 19.5 %pmax.7 = f32[1,128]{1,0:T(1,128)S(1)} all-reduce(f32[1,128]{1,0:T(1,128)S(1)} %get-tuple-element.113), channel_id=1, replica_groups=mesh['batch'=2,'freq'=8,'elem'=2] {'freq'}, use_global_device_ids=true, to_apply=%region_5.6 | all-reduce | flops 128 | bytes 1024 | tf_op jit(solution)/shard_map/pmax | solution.py:135
  (48 shorter events, 8.4 us)
Async XLA Ops:
  7.2 14.1 %copy-start = (f32[256,256]{1,0:T(8,128)S(1)}, f32[256,256]{1,0:T(8,128)}, u32[]{:S(2)}) copy-start(f32[256,256]{1,0:T(8,128)} %param.13) | copy-start | bytes 786436
  7.2 56.5 %all-reduce.3.cloned.1.call-start = ((), (), s32[]{:S(2)}) async-start(), calls=%async_computation.1 | async-start | bytes 4194304
  39.5 0.7 copy-start.2
  67.2 32.0 %all-to-all-start = ((bf16[1,16,2,128,128]{4,1,0,2,3:T(8,128)(2,1)}), bf16[1,16,2,128,128]{4,1,0,2,3:T(8,128)(2,1)S(1)}, u32[]{:S(2)}, u32[]{:S(2)}) async-start(bf16[1,16,2,128,128]{4,1,0,2,3:T(8,128)(2,1)} %copy.31), calls=%async_computation | async-start | bytes 2097152 | tf_op jit(solution)/shard_map/all_to_all | solution.py:133
  100.2 23.0 %copy-start.1 = (f32[1,16]{1,0:T(1,128)S(1)}, f32[1,16]{1,0:T(1,128)}, u32[]{:S(2)}) copy-start(f32[1,16]{1,0:T(1,128)} %param.17) | copy-start | bytes 196
Sparse Core Ops, SparseCore 0:
  39.7 23.9 all-reduce.2
where the time goes:
time: 131 us
  waiting for transfers between devices  49.1 us (37%)
  other arithmetic  20.2 us (15%)
  blocking collectives  19.5 us (15%)
  local copies, waits for them, and re-layouts  18.6 us (14%)
  between operations  14.2 us (11%)
  starting transfers between devices  5.81 us (4%)
  matrix products  3.2 us (2%)
    all_to_all x1, waiting for transfers between devices, body(): lax.all_to_all(summed, 'freq', split_axis=3, concat_axis=1, tiled=True)  26.2 us
    unnamed x2, waiting for transfers between devices  22.9 us
    pmax x1, blocking collectives, body(): whole_peak = lax.pmax(partial_peak, 'freq')  19.5 us
    another operation x1, other arithmetic  7.81 us
    unnamed x9, local copies, waits for them, and re-layouts  6.63 us
    all_to_all x1, starting transfers between devices, body(): lax.all_to_all(summed, 'freq', split_axis=3, concat_axis=1, tiled=True)  5.78 us
    gather x2, local copies, waits for them, and re-layouts, body(): jnp.take(beam_field, flaw_cells, axis=3)  5.75 us
  transfers between devices with their start and end apart: 2, of which 2 were waited for; matrix products, arithmetic and copies ran while one was open for 0% of the time, Pallas kernels for 0%

commit v1 on v0

--- a/solution.py
+++ b/solution.py
@@ -130,7 +130,12 @@
         rounded_term.astype(jnp.bfloat16), "elem", scatter_dimension=0, tiled=True
     )
     partial_peak = regroup_peaks(
-        lax.all_to_all(summed, "freq", split_axis=3, concat_axis=1, tiled=True)
+        jnp.concatenate(
+            lax.all_to_all(
+                jnp.stack(jnp.split(summed, lax.axis_size("freq"), axis=3)), "freq", 0, 0
+            ),
+            axis=1,
+        )
     )
     whole_peak = lax.pmax(partial_peak, "freq")
     columns = FG // freq_count

time: 131 us -> 136 us (1.038)
  local copies, waits for them, and re-layouts: 18.6 us -> 23.7 us
    another operation x0 -> x2, local copies, waits for them, and re-layouts: none -> 2.76 us  [the longest x1 2.27 us: body(): jnp.stack(jnp.split(summed, lax.axis_size('freq'), axis=3))]
    unnamed x9 -> x15, local copies, waits for them, and re-layouts: 6.63 us -> 9.36 us
where the time goes in v1:
time: 136 us
  waiting for transfers between devices  49.1 us (36%)
  local copies, waits for them, and re-layouts  23.7 us (17%)
  other arithmetic  20.2 us (15%)
  blocking collectives  19.5 us (14%)
  between operations  14.2 us (10%)
  starting transfers between devices  5.81 us (4%)
  matrix products  3.2 us (2%)
    all_to_all x1, waiting for transfers between devices, body(): lax.all_to_all(jnp.stack(jnp.split(summed, lax.axis_size('freq'), axis=3)...  26.2 us
    unnamed x2, waiting for transfers between devices  22.9 us
    pmax x1, blocking collectives, body(): whole_peak = lax.pmax(partial_peak, 'freq')  19.5 us
    unnamed x15, local copies, waits for them, and re-layouts  9.36 us
    another operation x1, other arithmetic  7.81 us
    all_to_all x1, starting transfers between devices, body(): lax.all_to_all(jnp.stack(jnp.split(summed, lax.axis_size('freq'), axis=3)...  5.78 us
    gather x2, local copies, waits for them, and re-layouts, body(): jnp.take(beam_field, flaw_cells, axis=3)  5.76 us
  transfers between devices with their start and end apart: 2, of which 2 were waited for; matrix products, arithmetic and copies ran while one was open for 0% of the time, Pallas kernels for 0%

profile of v1, /device:TPU:0, one launch (start us, length us, event | category | flops | bytes accessed | tf_op | source)
XLA Modules:
  0.0 135.8 jit_solution(12490831925255874524)
XLA Ops:
  7.2 0.7 compare_select_fusion.3
  7.9 1.2 compare_and_fusion
  10.1 0.7 compare_select_fusion
  10.8 0.7 and_bitcast_fusion
  11.5 3.5 %copy.47 = bf16[16,2,128,256]{2,0,3,1:T(8,128)(2,1)S(1)} copy(bf16[16,2,128,256]{3,2,1,0:T(8,128)(2,1)} %param.14) | data formatting | bytes 4194304 | tf_op args[4]
  15.0 2.3 %gather_fusion.2 = bf16[256,16,2,128]{3,1,2,0:T(8,128)(2,1)} fusion(bf16[16,2,128,256]{2,0,3,1:T(8,128)(2,1)S(1)} %copy.47, s32[1024]{0:T(1024)S(1)} %get-tuple-element.152), kind=kCustom, calls=%fused_computation.2 | custom fusion | bytes 4195328 | tf_op jit(solution)/shard_map/jit(_take)/gather | solution.py:118
  17.3 3.5 %copy.49 = bf16[16,2,128,2,128]{4,2,0,3,1:T(8,128)(2,1)S(1)} copy(bf16[16,2,128,2,128]{2,0,1,4,3:T(8,128)(2,1)} %bitcast.122) | data formatting | bytes 4194304 | tf_op jit(solution)/shard_map/jit(_take)/gather | solution.py:118
  21.3 0.8 gather_fusion
  22.1 1.4 %broadcast_select_fusion.3 = f32[128,256]{1,0:T(8,128)} fusion(f32[128,256]{1,0:T(8,128)S(1)} %gather_fusion, pred[128]{0:T(512)(128)(4,1)} %compare_and_fusion), kind=kLoop, calls=%fused_computation.81 | loop fusion | flops 32768 | bytes 262272 | tf_op jit(solution)/shard_map/jit(_take)/select_n | solution.py:116
  23.5 1.0 copy.46
  25.0 1.3 gather_fusion.1
  26.3 1.0 broadcast_select_fusion.2
  27.4 7.8 %fusion.30 = (bf16[16,2,128,128]{3,2,0,1:T(8,128)(2,1)S(1)}, bf16[16,2,128,128]{3,2,0,1:T(8,128)(2,1)S(1)}) fusion(f32[2,128,128]{2,1,0:T(8,128)S(1)} %broadcast_select_fusion.2, f32[16]{0:T(128)S(1)} %convert_multiply_fusion), kind=kLoop, calls=%fused_computation.49 | loop fusion | flops 2097152 | bytes 2228288 | tf_op jit(solution)/shard_map/convert.4
  35.2 0.7 broadcast_multiply_fusion.1
  36.0 1.4 %fusion.22 = f32[2,16,128,256]{3,2,1,0:T(8,128)S(1)} fusion(bf16[16,128,2,128]{3,1,0,2:T(8,128)(2,1)S(1)} %get-tuple-element.144, bf16[16,128,2,128]{3,1,0,2:T(8,128)(2,1)S(1)} %fusion.50, bf16[16,128,2,128]{3,1,0,2:T(8,128)(2,1)S(1)} %get-tuple-element.143, bf16[16,2,128,128]{3,2,0,1:T(8,128)(2,1)S(1)} %get-tuple-element.146, ...), kind=kOutput, calls=%fused_computation.39 | convolution fusion | flops 557842432 | bytes 9437184 | tf_op jit(solution)/shard_map/wgre,wegf->gwrf/dot_general | solution.py:124
  38.1 1.5 %pad_maximum_fusion.1 = bf16[2,16,2,128,128]{4,3,1,0,2:T(8,128)(2,1)} fusion(bf16[2,16,1,128,128]{4,3,1,0,2:T(8,128)(2,1)S(1)} %get-tuple-element.142, bf16[2,16,1,128,128]{4,3,1,0,2:T(8,128)(2,1)S(1)} %get-tuple-element.141), kind=kLoop, calls=%fused_computation.55 | loop fusion | flops 1048576 | bytes 4194304 | tf_op jit(solution)/shard_map/stack | solution.py:43
  40.8 22.9 %all-reduce.3.cloned.1.call-done = bf16[2,16,2,128,128]{4,3,1,0,2:T(8,128)(2,1)} async-done(((bf16[2,16,2,128,128]{4,3,1,0,2:T(8,128)(2,1)}), bf16[2,16,2,128,128]{4,3,1,0,2:T(8,128)(2,1)}) %all-reduce.3.cloned.1.call-update) | async-done | bytes 2097168
  63.7 1.9 %dynamic-slice_bitcast_fusion = bf16[1,16,2,128,128]{4,3,1,2,0:T(8,128)(2,1)S(1)} fusion(bf16[2,16,2,128,128]{4,3,1,0,2:T(8,128)(2,1)} %all-reduce.3.cloned.1.call-done, u32[]{:T(128)} %bitcast.47), kind=kLoop, calls=%fused_computation.63 | loop fusion | bytes 2097156 | tf_op jit(solution)/shard_map/reduce_scatter | solution.py:129
  68.3 0.7 fusion.41
  70.3 2.3 %fusion.38 = bf16[8,1,16,2,16,128]{5,4,2,3,1,0:T(8,128)(2,1)} fusion(bf16[8,1,16,2,16,128]{5,4,2,3,1,0:T(8,128)(2,1)} %fusion.39, bf16[2,16,2,128,128]{4,3,1,0,2:T(8,128)(2,1)} %all-reduce.3.cloned.1.call-done, u32[]{:T(128)} %bitcast.47, u32[]{:T(128)S(6)} %convert.21), kind=kLoop, calls=%fused_computation.65 | loop fusion | bytes 262660 | tf_op jit(solution)/shard_map/stack | solution.py:135
  72.6 5.8 %all-to-all-start = ((bf16[8,1,16,2,16,128]{5,4,2,3,1,0:T(8,128)(2,1)}), bf16[8,1,16,2,16,128]{5,4,2,3,1,0:T(8,128)(2,1)S(1)}, u32[]{:S(2)}, u32[]{:S(2)}) async-start(bf16[8,1,16,2,16,128]{5,4,2,3,1,0:T(8,128)(2,1)} %fusion.38), calls=%async_computation | async-start | bytes 2097152 | tf_op jit(solution)/shard_map/all_to_all | solution.py:134
  78.3 26.2 %all-to-all-done = bf16[8,1,16,2,16,128]{5,4,2,3,1,0:T(8,128)(2,1)S(1)} async-done(((bf16[8,1,16,2,16,128]{5,4,2,3,1,0:T(8,128)(2,1)}), bf16[8,1,16,2,16,128]{5,4,2,3,1,0:T(8,128)(2,1)S(1)}, u32[]{:S(2)}, u32[]{:S(2)}) %all-to-all-start) | async-done | bytes 1048608 | tf_op jit(solution)/shard_map/all_to_all | solution.py:134
  105.3 3.5 %while.16 = (s32[]{:T(128)}, f32[1,128]{1,0:T(1,128)S(1)}, bf16[1,128,2,2048]{3,1,2,0:T(8,128)(2,1)S(1)}, s32[]{:T(128)}, s32[]{:T(128)}, /*index=5*/s32[]{:T(128)}) while((s32[]{:T(128)}, f32[1,128]{1,0:T(1,128)S(1)}, bf16[1,128,2,2048]{3,1,2,0:T(8,128)(2,1)S(1)}, s32[]{:T(128)}, s32[]{:T(128)}, /*index=5*/s32[]{:T(128)}) %tuple.59), condition=%wide.region_4.5_spmd.clone, body=%wide.region_1.4_spmd.clone.sunk | while | flops 539607296 | bytes 12078175 | solution.py:83
  108.9 19.5 %pmax.7 = f32[1,128]{1,0:T(1,128)S(1)} all-reduce(f32[1,128]{1,0:T(1,128)S(1)} %get-tuple-element.113), channel_id=1, replica_groups=mesh['batch'=2,'freq'=8,'elem'=2] {'freq'}, use_global_device_ids=true, to_apply=%region_5.6 | all-reduce | flops 128 | bytes 1024 | tf_op jit(solution)/shard_map/pmax | solution.py:140
  (54 shorter events, 12.9 us)
Async XLA Ops:
  7.2 14.2 %copy-start = (f32[256,256]{1,0:T(8,128)S(1)}, f32[256,256]{1,0:T(8,128)}, u32[]{:S(2)}) copy-start(f32[256,256]{1,0:T(8,128)} %param.13) | copy-start | bytes 786436
  7.2 56.5 %all-reduce.3.cloned.1.call-start = ((), (), s32[]{:S(2)}) async-start(), calls=%async_computation.1 | async-start | bytes 4194304
  39.6 0.7 copy-start.2
  72.6 32.0 %all-to-all-start = ((bf16[8,1,16,2,16,128]{5,4,2,3,1,0:T(8,128)(2,1)}), bf16[8,1,16,2,16,128]{5,4,2,3,1,0:T(8,128)(2,1)S(1)}, u32[]{:S(2)}, u32[]{:S(2)}) async-start(bf16[8,1,16,2,16,128]{5,4,2,3,1,0:T(8,128)(2,1)} %fusion.38), calls=%async_computation | async-start | bytes 2097152 | tf_op jit(solution)/shard_map/all_to_all | solution.py:134
  105.3 23.0 %copy-start.1 = (f32[1,16]{1,0:T(1,128)S(1)}, f32[1,16]{1,0:T(1,128)}, u32[]{:S(2)}) copy-start(f32[1,16]{1,0:T(1,128)} %param.17) | copy-start | bytes 196
Sparse Core Ops, SparseCore 0:
  39.7 23.9 all-reduce.2
